TPU v7x, 512 devices: a whole 4x8x8 slice. The times are simulated.
512 devices in a mesh: ep: 32 (over y, x), tp: 16 (over z, core).
Axes of the slice: x: 4, y: 8, z: 8, core: 2. Of those that a mesh axis runs over, the one named last changes fastest.
Arguments:
- quantized: bfloat16 [32, 4096, 2048], P('ep', None, 'tp'), may hold values from -4 to 4
- block_scale: bfloat16 [32, 32, 16], P('ep', None, 'tp'), may hold values from 0.01 to 1
- slot_expert: int32 [64], replicated, may hold values from 0 to 31, as said below
Outputs:
- serving: bfloat16 [64, 4096, 2048], P('ep', None, 'tp')
- tensor_scale: float32 [64], P('ep')
Inputs may be any that keep to these rules, and one draw needn't show every extreme that they name: `slot_expert`: slot j belongs to the holder of index j // 2 of ep; every expert has at least one slot, and an expert may have several.
All inputs are finite; a program needn't handle non-finite values. Where the computation divides by a largest or mean magnitude, that divisor is 1e-20 or more.
Results may differ from a plain program's by a relative error of at most 0.001.
Values may be sent and summed in bfloat16 or wider, within the bound.
A program may use at most 64 MiB of HBM per device.

v0:
```python
import math

import jax
import jax.numpy as jnp
from jax import lax
from jax.sharding import PartitionSpec as P

BLOCK = 128


EPSILON = 1e-06


def hadamard(length):
    indices = jnp.arange(length, dtype=jnp.int32)
    common = indices[:, None] & indices[None, :]
    parity = jnp.zeros((length, length), jnp.int32)
    for position in range(length.bit_length() - 1):
        parity = parity + (common >> position & 1)
    return (1 - 2 * (parity % 2)).astype(jnp.float32) / math.sqrt(length)


def rotate_blocks(values, scales):
    count, row_count, col_count = values.shape
    blocks = values.astype(jnp.float32).reshape(
        count, row_count // BLOCK, BLOCK, col_count // BLOCK, BLOCK
    )
    blocks = blocks * scales.astype(jnp.float32)[:, :, None, :, None]
    return jnp.einsum("eiajb,bc->eiajc", blocks, hadamard(BLOCK), precision=lax.Precision.HIGHEST)


def normalize(rotated, largest):
    count, row_blocks, width_a, col_blocks, width_b = rotated.shape
    scaled = rotated / (largest + EPSILON)[:, None, None, None, None]
    return scaled.reshape(count, row_blocks * width_a, col_blocks * width_b).astype(jnp.bfloat16)


def on_device(quantized, block_scale, slot_expert):
    rows_vals, rows_scales = (
        lax.all_to_all(quantized, "ep", split_axis=1, concat_axis=0, tiled=True),
        lax.all_to_all(block_scale, "ep", split_axis=1, concat_axis=0, tiled=True),
    )
    picked_vals = jnp.take(rows_vals, slot_expert, axis=0)
    picked_scales = jnp.take(rows_scales, slot_expert, axis=0)
    slot_vals, slot_scales = (
        lax.all_to_all(picked_vals, "ep", split_axis=0, concat_axis=1, tiled=True),
        lax.all_to_all(picked_scales, "ep", split_axis=0, concat_axis=1, tiled=True),
    )
    rotated = rotate_blocks(slot_vals, slot_scales)
    local_max = jnp.max(jnp.abs(rotated), axis=(1, 2, 3, 4))
    largest = lax.pmax(local_max, "tp")
    serving = normalize(rotated, largest)
    return (serving, largest)


def solution(mesh):
    in_specs = (P("ep", None, "tp"), P("ep", None, "tp"), P())
    out_specs = (P("ep", None, "tp"), P("ep"))
    return jax.shard_map(
        on_device, mesh=mesh, in_specs=in_specs, out_specs=out_specs, check_vma=False
    )
```

profile of v0, /device:TPU:6, one launch (start us, length us, event | category | flops | bytes accessed | tf_op | source)
XLA Modules:
  0.0 183.1 jit_solution(16278711069579966444)
XLA Ops:
  0.6 1.3 copy.16
  2.0 10.2 %all-to-all-start.2 = ((bf16[1,32,1]{2,0,1:T(2,128)(2,1)}), bf16[1,32,1]{2,0,1:T(2,128)(2,1)S(1)}, u32[]{:S(2)}, u32[]{:S(2)}) async-start(bf16[1,32,1]{2,0,1:T(2,128)(2,1)} %copy.16), calls=%async_computation.2 | async-start | bytes 32768 | tf_op jit(solution)/shard_map/all_to_all | solution.py:41
  12.2 3.2 %copy.29 = bf16[1,4096,128]{2,0,1:T(2,128)(2,1)S(1)} copy(bf16[1,4096,128]{2,1,0:T(8,128)(2,1)} %param.3) | data formatting | bytes 2097152 | tf_op args[0]
  15.4 0.5 broadcast.49
  15.9 22.4 %reduce.5 = bf16[4096,128]{1,0:T(8,128)(2,1)S(1)} reduce(bf16[4096,1,128]{2,1,0:T(2,128)(2,1)S(1)} %bitcast.28, bf16[]{:T(256)} %broadcast.49), dimensions={1}, to_apply=%bitcast.25.reduce_sub_computation | reduce | bytes 2097154
  38.3 1.1 reshape.86
  39.4 9.8 %all-to-all-start = ((bf16[32,2,8192]{2,1,0:T(2,128)(2,1)}), bf16[32,2,8192]{2,1,0:T(2,128)(2,1)S(1)}, u32[]{:S(2)}, u32[]{:S(2)}) async-start(bf16[32,2,8192]{2,1,0:T(2,128)(2,1)} %reshape.86), calls=%async_computation | async-start | bytes 2097152 | tf_op jit(solution)/shard_map/all_to_all | solution.py:40
  49.2 0.3 reduce.2
  49.5 0.8 gather_fusion.1
  50.3 0.7 copy.17
  51.0 25.6 %all-to-all-done = bf16[32,2,8192]{2,1,0:T(2,128)(2,1)S(1)} async-done(((bf16[32,2,8192]{2,1,0:T(2,128)(2,1)}), bf16[32,2,8192]{2,1,0:T(2,128)(2,1)S(1)}, u32[]{:S(2)}, u32[]{:S(2)}) %all-to-all-start) | async-done | bytes 1048608 | tf_op jit(solution)/shard_map/all_to_all | solution.py:40
  76.7 5.6 %all-to-all-start.3 = ((bf16[64,1,1]{2,1,0:T(2,128)(2,1)}), bf16[64,1,1]{2,1,0:T(2,128)(2,1)S(1)}, u32[]{:S(2)}, u32[]{:S(2)}) async-start(bf16[64,1,1]{2,1,0:T(2,128)(2,1)} %copy.17), calls=%async_computation.3 | async-start | bytes 65536 | tf_op jit(solution)/shard_map/all_to_all | solution.py:47
  82.3 1.1 reshape.87
  83.3 0.1 copy.23
  83.5 1.0 gather_fusion
  84.4 1.6 broadcast_select_fusion
  86.0 4.4 %all-to-all-done.3 = bf16[64,1,1]{2,1,0:T(2,128)(2,1)S(1)} async-done(((bf16[64,1,1]{2,1,0:T(2,128)(2,1)}), bf16[64,1,1]{2,1,0:T(2,128)(2,1)S(1)}, u32[]{:S(2)}, u32[]{:S(2)}) %all-to-all-start.3) | async-done | bytes 160 | tf_op jit(solution)/shard_map/all_to_all | solution.py:47
  90.4 5.6 %all-to-all-start.1 = ((bf16[64,128,128]{2,1,0:T(8,128)(2,1)}), bf16[64,128,128]{2,1,0:T(8,128)(2,1)S(1)}, u32[]{:S(2)}, u32[]{:S(2)}) async-start(bf16[64,128,128]{2,1,0:T(8,128)(2,1)} %broadcast_select_fusion), calls=%async_computation.1 | async-start | bytes 4194304 | tf_op jit(solution)/shard_map/all_to_all | solution.py:46
  96.0 0.6 convert_reduce_fusion
  96.6 0.1 reshape.56
  96.7 47.1 %all-to-all-done.1 = bf16[64,128,128]{2,1,0:T(8,128)(2,1)S(1)} async-done(((bf16[64,128,128]{2,1,0:T(8,128)(2,1)}), bf16[64,128,128]{2,1,0:T(8,128)(2,1)S(1)}, u32[]{:S(2)}, u32[]{:S(2)}) %all-to-all-start.1) | async-done | bytes 2097184 | tf_op jit(solution)/shard_map/all_to_all | solution.py:46
  143.8 5.1 %abs_reduce_fusion = (f32[2]{0:T(128)S(1)}, f32[2,32,128,128]{3,2,1,0:T(8,128)}) fusion(bf16[32,2,128,128]{3,2,1,0:T(8,128)(2,1)S(1)} %bitcast.30, f32[2,32]{0,1:T(8,128)S(1)} %bitcast.31), kind=kOutput, calls=%fused_computation.7 | convolution fusion | flops 1615396864 | bytes 6291720 | tf_op jit(solution)/shard_map/eiajb,bc->eiajc/dot_general | solution.py:29
  148.9 30.1 %pmax.7 = f32[2]{0:T(128)S(1)} all-reduce(f32[2]{0:T(128)S(1)} %get-tuple-element.4), channel_id=1, replica_groups=mesh['ep'=32,'tp'=16] {'tp'}, use_global_device_ids=true, to_apply=%region_1.2 | all-reduce | flops 2 | bytes 16 | tf_op jit(solution)/shard_map/pmax | solution.py:51
  179.0 4.1 %divide_convert_fusion = bf16[2,32,128,128]{3,2,1,0:T(8,128)(2,1)} fusion(f32[2,32,128,128]{3,2,1,0:T(8,128)} %get-tuple-element.5, f32[2]{0:T(128)S(1)} %broadcast_add_fusion), kind=kLoop, calls=%fused_computation.6 | loop fusion | flops 2097152 | bytes 6291464 | tf_op jit(solution)/shard_map/convert_element_type | solution.py:35
  (9 shorter events, 0.0 us)
Async XLA Ops:
  2.0 37.4 %all-to-all-start.2 = ((bf16[1,32,1]{2,0,1:T(2,128)(2,1)}), bf16[1,32,1]{2,0,1:T(2,128)(2,1)S(1)}, u32[]{:S(2)}, u32[]{:S(2)}) async-start(bf16[1,32,1]{2,0,1:T(2,128)(2,1)} %copy.16), calls=%async_computation.2 | async-start | bytes 32768 | tf_op jit(solution)/shard_map/all_to_all | solution.py:41
  38.3 10.9 %copy-start = (s32[64]{0:T(128)S(1)}, s32[64]{0:T(128)}, u32[]{:S(2)}) copy-start(s32[64]{0:T(128)} %param.5) | copy-start | bytes 772
  39.4 37.3 %all-to-all-start = ((bf16[32,2,8192]{2,1,0:T(2,128)(2,1)}), bf16[32,2,8192]{2,1,0:T(2,128)(2,1)S(1)}, u32[]{:S(2)}, u32[]{:S(2)}) async-start(bf16[32,2,8192]{2,1,0:T(2,128)(2,1)} %reshape.86), calls=%async_computation | async-start | bytes 2097152 | tf_op jit(solution)/shard_map/all_to_all | solution.py:40
  76.7 13.7 %all-to-all-start.3 = ((bf16[64,1,1]{2,1,0:T(2,128)(2,1)}), bf16[64,1,1]{2,1,0:T(2,128)(2,1)S(1)}, u32[]{:S(2)}, u32[]{:S(2)}) async-start(bf16[64,1,1]{2,1,0:T(2,128)(2,1)} %copy.17), calls=%async_computation.3 | async-start | bytes 65536 | tf_op jit(solution)/shard_map/all_to_all | solution.py:47
  90.4 53.4 %all-to-all-start.1 = ((bf16[64,128,128]{2,1,0:T(8,128)(2,1)}), bf16[64,128,128]{2,1,0:T(8,128)(2,1)S(1)}, u32[]{:S(2)}, u32[]{:S(2)}) async-start(bf16[64,128,128]{2,1,0:T(8,128)(2,1)} %broadcast_select_fusion), calls=%async_computation.1 | async-start | bytes 4194304 | tf_op jit(solution)/shard_map/all_to_all | solution.py:46
  179.0 4.1 %copy-start.1 = (f32[2]{0:T(128)}, f32[2]{0:T(128)S(1)}, u32[]{:S(2)}) copy-start(f32[2]{0:T(128)S(1)} %pmax.7) | copy-start | bytes 28
where the time goes:
time: 184 us; the launch traced here: 183 us
  waiting for transfers between devices  77.2 us (42%)
  starting transfers between devices  31.1 us (17%)
  blocking collectives  30.1 us (16%)
  other arithmetic  29 us (16%)
  local copies, waits for them, and re-layouts  9.89 us (5%)
  matrix products  5.1 us (3%)
    all_to_all x1, waiting for transfers between devices, on_device(): lax.all_to_all(picked_vals, 'ep', split_axis=0, concat_axis=1, tiled=True)  47.1 us
    pmax x1, blocking collectives, on_device(): largest = lax.pmax(local_max, 'tp')  30.1 us
    all_to_all x1, waiting for transfers between devices, on_device(): lax.all_to_all(quantized, 'ep', split_axis=1, concat_axis=0, tiled=True)  25.6 us
    unnamed x1, other arithmetic  22.4 us
    all_to_all x1, starting transfers between devices, on_device(): lax.all_to_all(block_scale, 'ep', split_axis=1, concat_axis=0, tiled=True)  10.2 us
    all_to_all x1, starting transfers between devices, on_device(): lax.all_to_all(quantized, 'ep', split_axis=1, concat_axis=0, tiled=True)  9.78 us
    unnamed x10, local copies, waits for them, and re-layouts  7.34 us
    all_to_all x1, starting transfers between devices, on_device(): lax.all_to_all(picked_vals, 'ep', split_axis=0, concat_axis=1, tiled=True)  5.61 us
  transfers between devices with their start and end apart: 4, of which 3 were waited for; matrix products, arithmetic and copies ran while one was open for 18% of the time, Pallas kernels for 0%

commit v1 on v0

v1 whole, which is shorter than its diff:
```python
import functools
import math

import jax
import jax.numpy as jnp
from jax import lax
from jax.experimental import pallas as pl
from jax.experimental.pallas import tpu as pltpu
from jax.sharding import PartitionSpec as P

MESH = pl.DeviceIdType.MESH
BLOCK = 128
EPSILON = 1e-06
NX, NY = 4, 8
EP = NX * NY
REACH = 4
STAGES = 4
PIECE = BLOCK // STAGES
HALF = REACH * NX


def sign_matrix():
    rows = lax.broadcasted_iota(jnp.int32, (BLOCK, BLOCK), 0)
    cols = lax.broadcasted_iota(jnp.int32, (BLOCK, BLOCK), 1)
    common = rows & cols
    common = common ^ (common >> 4)
    common = common ^ (common >> 2)
    common = common ^ (common >> 1)
    return (1 - 2 * (common & 1)).astype(jnp.float32).astype(jnp.bfloat16)


def to_column(row, count):
    spread = jnp.broadcast_to(row, (count, BLOCK))
    at_row = lax.broadcasted_iota(jnp.int32, (count, BLOCK), 0)
    at_lane = lax.broadcasted_iota(jnp.int32, (count, BLOCK), 1)
    return jnp.sum(jnp.where(at_row == at_lane, spread, 0.0), axis=1, keepdims=True)


def move_kernel(
    tp_bits,
    slot_ref,
    stored_ref,
    scale_ref,
    raw_ref,
    table_ref,
    own,
    signs,
    picked,
    block_max,
    peer_out,
    peer_in,
    row_out,
    own_sem,
    near_sem,
    far_sem,
    in_sem,
    row_sem,
    peer_sem,
    send_near,
    send_far,
    send_in,
    send_row,
    send_peer,
    *held_refs,
):
    held = (held_refs[:STAGES], held_refs[STAGES:])
    me = lax.axis_index("ep")
    tp = lax.axis_index("tp")
    here_y, here_x = me // NX, lax.rem(me, NX)
    row_blocks = stored_ref.shape[0] // BLOCK

    barrier = pltpu.get_barrier_semaphore()

    def greet(step, _):
        pl.semaphore_signal(
            barrier, inc=1, device_id=(lax.rem(me + step, EP), tp), device_id_type=MESH
        )
        return _

    lax.fori_loop(1, EP, greet, 0)
    for bit in range(tp_bits):
        pl.semaphore_signal(
            barrier, inc=1, device_id=(me, tp ^ (1 << bit)), device_id_type=MESH
        )
    pl.semaphore_wait(barrier, EP - 1 + tp_bits)

    own_copy = pltpu.make_async_copy(stored_ref, own, own_sem)

    def near_rows(side, reach, stage):
        to_y = lax.rem(here_y + (NY + reach if side == 0 else NY - reach), NY)
        chunk = lax.rem(to_y + NY - side, NY)
        return to_y, chunk

    def near_copy(side, reach, dx, stage):
        to_y, chunk = near_rows(side, reach, stage)
        to_x = lax.rem(here_x + dx, NX)
        start = pl.multiple_of((chunk * NX + to_x) * BLOCK + stage * PIECE, PIECE)
        return (
            stored_ref.at[pl.ds(start, PIECE)],
            held[side][stage].at[reach * NX + here_x],
            (to_y * NX + to_x, tp),
        )

    for stage in range(STAGES):
        for side in range(2):
            source, target, _ = near_copy(side, 0, 0, stage)
            pltpu.make_async_copy(source, target, near_sem.at[side, stage]).start()

        def send_one(step, _, stage=stage):
            for side in range(2):
                source, target, device = near_copy(side, step // NX, lax.rem(step, NX), stage)
                pltpu.make_async_remote_copy(
                    src_ref=source,
                    dst_ref=target,
                    send_sem=send_near,
                    recv_sem=near_sem.at[side, stage],
                    device_id=device,
                    device_id_type=MESH,
                ).start()
            return _

        lax.fori_loop(1, HALF, send_one, 0)

    own_copy.start()
    signs[...] = sign_matrix()
    own_copy.wait()

    def one_block(index, _):
        rows = own[pl.ds(pl.multiple_of(index * BLOCK, BLOCK), BLOCK), :]
        turned = jnp.dot(rows, signs[...], preferred_element_type=jnp.float32)
        block_max[pl.ds(index, 1), :] = jnp.max(jnp.abs(turned), axis=0, keepdims=True)
        return _

    lax.fori_loop(0, row_blocks, one_block, 0)

    row_out[...] = jnp.zeros_like(row_out)
    row_out[0, :, 0:row_blocks] = scale_ref[...].astype(jnp.float32)
    scale_row = row_out[0, :, :]
    largest = jnp.max(block_max[...] * to_column(scale_row, row_blocks)) * (1.0 / math.sqrt(BLOCK))

    def peer_copy(bit):
        return pltpu.make_async_remote_copy(
            src_ref=peer_out.at[bit],
            dst_ref=peer_in.at[bit],
            send_sem=send_peer.at[bit],
            recv_sem=peer_sem.at[bit],
            device_id=(me, tp ^ (1 << bit)),
            device_id_type=MESH,
        )

    def peer_start(bit, value):
        peer_out[bit] = value
        peer_copy(bit).start()

    def peer_finish(bit):
        peer_copy(bit).wait()
        return jnp.maximum(peer_out[bit], peer_in[bit])

    state = {"value": jnp.full((8, BLOCK), largest, jnp.float32), "bit": 0}

    def row_copy(step):
        return pltpu.make_async_remote_copy(
            src_ref=row_out.at[0],
            dst_ref=table_ref.at[me],
            send_sem=send_row,
            recv_sem=row_sem,
            device_id=(lax.rem(me + step, EP), tp),
            device_id_type=MESH,
        )

    def send_rows(value):
        lane = lax.broadcasted_iota(jnp.int32, (1, BLOCK), 1)
        row_out[0, :, :] = jnp.where(lane < row_blocks, scale_row, value[0:1, :])
        pltpu.make_async_copy(row_out.at[0], table_ref.at[me], row_sem).start()

        def send_row_to(step, _):
            row_copy(step).start()
            return _

        lax.fori_loop(1, EP, send_row_to, 0)

    def advance():
        bit = state["bit"]
        if bit > 0 and bit <= tp_bits:
            state["value"] = peer_finish(bit - 1)
        if bit < tp_bits:
            peer_start(bit, state["value"])
        if bit == tp_bits:
            send_rows(state["value"])
        state["bit"] = bit + 1

    def far_copy(side, stage):
        to_y = lax.rem(here_y + (1 if side == 0 else NY - 1), NY)
        return pltpu.make_async_remote_copy(
            src_ref=held[side][stage].at[pl.ds(0, HALF)],
            dst_ref=held[1 - side][stage].at[pl.ds(HALF, HALF)],
            send_sem=send_far,
            recv_sem=far_sem.at[1 - side, stage],
            device_id=(to_y * NX + here_x, tp),
            device_id_type=MESH,
        )

    advance()
    for stage in range(STAGES):
        for side in range(2):
            arrived = held[side][stage].at[pl.ds(0, HALF)]
            pltpu.make_async_copy(arrived, arrived, near_sem.at[side, stage]).wait()
            far_copy(side, stage).start()
        advance()

    def in_target(side, step, stage):
        reach, dx = step // NX, lax.rem(step, NX)
        to_y = lax.rem(here_y + (NY - reach if side == 0 else NY + reach), NY)
        return to_y * NX + lax.rem(here_x + dx, NX)

    def in_rows(side, stage):
        chunk = lax.rem(here_y + NY - side, NY)
        start = pl.multiple_of((chunk * NX + here_x) * BLOCK + stage * PIECE, PIECE)
        return raw_ref.at[:, pl.ds(start, PIECE)]

    for stage in range(STAGES):
        for side in range(2):
            arrived = held[side][stage].at[pl.ds(HALF, HALF)]
            pltpu.make_async_copy(arrived, arrived, far_sem.at[side, stage]).wait()

            def pick(step, _, side=side, stage=stage):
                device = in_target(side, step, stage)
                for slot in range(2):
                    expert = slot_ref[2 * device + slot]
                    from_y, from_x = expert >> 2, expert & 3
                    away = (here_y - from_y if side == 0 else from_y - here_y) & 7
                    index = jnp.where(away < REACH, away, HALF // NX + 7 - away) * NX + from_x
                    picked[stage, side * HALF + step, slot] = held[side][stage][index]
                return _

            lax.fori_loop(0, HALF, pick, 0)

            local = picked.at[stage, side * HALF]
            pltpu.make_async_copy(local, in_rows(side, stage), in_sem.at[stage]).start()

            def send_in_one(step, _, side=side, stage=stage):
                pltpu.make_async_remote_copy(
                    src_ref=picked.at[stage, side * HALF + step],
                    dst_ref=in_rows(side, stage),
                    send_sem=send_in,
                    recv_sem=in_sem.at[stage],
                    device_id=(in_target(side, step, stage), tp),
                    device_id_type=MESH,
                ).start()
                return _

            lax.fori_loop(1, HALF, send_in_one, 0)
        advance()

    while state["bit"] <= tp_bits:
        advance()

    pltpu.make_async_copy(table_ref, table_ref, row_sem).wait()
    for stage in range(STAGES):
        part = raw_ref.at[:, pl.ds(0, EP * PIECE)]
        pltpu.make_async_copy(part, part, in_sem.at[stage]).wait()
    sent = table_ref.at[pl.ds(0, EP - 1)]
    pltpu.make_async_copy(sent, sent, send_row).wait()
    sent = own.at[pl.ds(0, 2 * (HALF - 1) * BLOCK)]
    pltpu.make_async_copy(sent, sent, send_near).wait()
    sent = own.at[pl.ds(0, 2 * HALF * BLOCK)]
    pltpu.make_async_copy(sent, sent, send_far).wait()
    sent = picked.at[:, pl.ds(0, 2 * (HALF - 1))]
    pltpu.make_async_copy(sent, sent, send_in).wait()


def move_rows(tp_bits, stored, scale, slot_expert):
    rows = stored.shape[0]
    row_blocks = rows // BLOCK
    dma = pltpu.SemaphoreType.DMA
    return pl.pallas_call(
        functools.partial(move_kernel, tp_bits),
        out_shape=(
            jax.ShapeDtypeStruct((2, rows, BLOCK), jnp.bfloat16),
            jax.ShapeDtypeStruct((EP, 1, BLOCK), jnp.float32),
        ),
        in_specs=[
            pl.BlockSpec(memory_space=pltpu.SMEM),
            pl.BlockSpec(memory_space=pl.ANY),
            pl.BlockSpec(memory_space=pltpu.VMEM),
        ],
        out_specs=(pl.BlockSpec(memory_space=pl.ANY), pl.BlockSpec(memory_space=pl.ANY)),
        scratch_shapes=[
            pltpu.VMEM((rows, BLOCK), jnp.bfloat16),
            pltpu.VMEM((BLOCK, BLOCK), jnp.bfloat16),
            pltpu.VMEM((STAGES, 2 * HALF, 2, PIECE, BLOCK), jnp.bfloat16),
            pltpu.VMEM((row_blocks, BLOCK), jnp.float32),
            pltpu.VMEM((max(tp_bits, 1), 8, BLOCK), jnp.float32),
            pltpu.VMEM((max(tp_bits, 1), 8, BLOCK), jnp.float32),
            pltpu.VMEM((1, 1, BLOCK), jnp.float32),
            dma,
            dma((2, STAGES)),
            dma((2, STAGES)),
            dma((STAGES,)),
            dma,
            dma((max(tp_bits, 1),)),
            dma,
            dma,
            dma,
            dma,
            dma((max(tp_bits, 1),)),
        ]
        + [pltpu.VMEM((2 * HALF, PIECE, BLOCK), jnp.bfloat16)] * (2 * STAGES),
        compiler_params=pltpu.CompilerParams(collective_id=0, has_side_effects=True),
        name="move_rows",
    )(slot_expert, stored, scale)


TILE = 1024


def finish_kernel(slot_ref, raw_ref, table_ref, out_ref, largest_ref, signs, factors):
    slot, tile = pl.program_id(0), pl.program_id(1)
    row_blocks = factors.shape[0]
    blocks = TILE // BLOCK

    @pl.when((slot == 0) & (tile == 0))
    def _():
        signs[...] = sign_matrix()

    @pl.when(tile == 0)
    def _():
        expert = slot_ref[2 * lax.axis_index("ep") + slot]
        row = table_ref[expert]
        lane = lax.broadcasted_iota(jnp.int32, (1, BLOCK), 1)
        largest = jnp.max(jnp.where(lane < row_blocks, 0.0, row))
        largest_ref[slot] = largest
        bound = jnp.full((row_blocks, BLOCK), largest, jnp.float32) + EPSILON
        scale = jnp.broadcast_to(to_column(row, row_blocks), (row_blocks, BLOCK))
        factors[...] = (scale * (1.0 / math.sqrt(BLOCK))) / bound

    for block in range(blocks):
        at = pl.ds(block * BLOCK, BLOCK)
        turned = jnp.dot(raw_ref[0, at, :], signs[...], preferred_element_type=jnp.float32)
        factor = factors[pl.ds(tile * blocks + block, 1), :]
        out_ref[0, at, :] = (turned * factor).astype(jnp.bfloat16)


def finish(raw, table, slot_expert):
    count, rows, width = raw.shape
    return pl.pallas_call(
        finish_kernel,
        grid=(count, rows // TILE),
        out_shape=(
            jax.ShapeDtypeStruct(raw.shape, jnp.bfloat16),
            jax.ShapeDtypeStruct((count,), jnp.float32),
        ),
        in_specs=[
            pl.BlockSpec(memory_space=pltpu.SMEM),
            pl.BlockSpec((1, TILE, width), lambda i, j: (i, j, 0)),
            pl.BlockSpec(memory_space=pltpu.VMEM),
        ],
        out_specs=(
            pl.BlockSpec((1, TILE, width), lambda i, j: (i, j, 0)),
            pl.BlockSpec(memory_space=pltpu.SMEM),
        ),
        scratch_shapes=[
            pltpu.VMEM((BLOCK, BLOCK), jnp.bfloat16),
            pltpu.VMEM((rows // BLOCK, BLOCK), jnp.float32),
        ],
        name="finish",
    )(slot_expert, raw, table)


def on_device(tp_bits, quantized, block_scale, slot_expert):
    rows = quantized.shape[1]
    stored = quantized.reshape(rows, BLOCK)
    scale = block_scale.reshape(1, rows // BLOCK)
    raw, table = move_rows(tp_bits, stored, scale, slot_expert)
    return finish(raw, table, slot_expert)


def solution(mesh):
    tp_bits = mesh.shape["tp"].bit_length() - 1
    in_specs = (P("ep", None, "tp"), P("ep", None, "tp"), P())
    out_specs = (P("ep", None, "tp"), P("ep"))
    return jax.shard_map(
        functools.partial(on_device, tp_bits),
        mesh=mesh,
        in_specs=in_specs,
        out_specs=out_specs,
        check_vma=False,
    )
```

time: 184 us -> 88.2 us (0.48)
  the two profiles are of different devices: /device:TPU:6 before, /device:TPU:8 now
where the time goes in v1:
time: 88.2 us; the launch traced here: 87.9 us
  Pallas kernels  87.3 us (99%)
    pallas_call x1, Pallas kernels, move_rows(): pl.pallas_call(functools.partial(move_kernel, tp_bits), out_shape=(jax.Sh...  80.5 us
    pallas_call x1, Pallas kernels, finish(): pl.pallas_call(finish_kernel, grid=(count, rows // TILE), out_shape=(jax....  6.74 us

profile of v1, /device:TPU:8, one launch (start us, length us, event | category | flops | bytes accessed | tf_op | source)
XLA Modules:
  0.0 87.9 jit_solution(15501340927916251440)
XLA Ops:
  0.6 80.5 %move_rows.1 = (bf16[2,4096,128]{2,1,0:T(8,128)(2,1)}, f32[32,1,128]{2,1,0:T(1,128)}) custom-call(s32[64]{0:T(128)} %slot_ref.3, bf16[4096,128]{1,0:T(8,128)(2,1)} %bitcast.2, bf16[1,32]{1,0:T(2,128)(2,1)} %bitcast.3), custom_call_target="tpu_custom_call" | custom-call | tf_op jit(solution)/shard_map/move_rows/pallas_call | solution.py:276
  81.1 6.7 %finish.1 = (bf16[2,4096,128]{2,1,0:T(8,128)(2,1)}, f32[2]{0:T(128)}) custom-call(s32[64]{0:T(128)} %slot_ref.3, bf16[2,4096,128]{2,1,0:T(8,128)(2,1)} %get-tuple-element.4.raw_ref, f32[32,1,128]{2,1,0:T(1,128)} %get-tuple-element.5.table_ref), custom_call_target="tpu_custom_call" | custom-call | tf_op jit(solution)/shard_map/finish/pallas_call | solution.py:346

commit v2 on v0

v2 whole, which is shorter than its diff:
```python
import functools
import math

import jax
import jax.numpy as jnp
from jax import lax
from jax.experimental import pallas as pl
from jax.experimental.pallas import tpu as pltpu
from jax.sharding import PartitionSpec as P

MESH = pl.DeviceIdType.MESH
BLOCK = 128
EPSILON = 1e-06
NX, NY = 4, 8
EP = NX * NY
HOLD = 4
OUT = (NY - HOLD) // 2
LAST = HOLD - 1
STAGES = 4
PIECE = BLOCK // STAGES
HUB = 0
VMEM_LIMIT = 16 << 20


def sign_matrix():
    rows = lax.broadcasted_iota(jnp.int32, (BLOCK, BLOCK), 0)
    cols = lax.broadcasted_iota(jnp.int32, (BLOCK, BLOCK), 1)
    common = rows & cols
    common = common ^ (common >> 4)
    common = common ^ (common >> 2)
    common = common ^ (common >> 1)
    return (1 - 2 * (common & 1)).astype(jnp.float32).astype(jnp.bfloat16)


def to_column(row, count):
    spread = jnp.broadcast_to(row, (count, BLOCK))
    at_row = lax.broadcasted_iota(jnp.int32, (count, BLOCK), 0)
    at_lane = lax.broadcasted_iota(jnp.int32, (count, BLOCK), 1)
    return jnp.sum(jnp.where(at_row == at_lane, spread, 0.0), axis=1, keepdims=True)


def move_kernel(
    tp_size,
    slot_hbm,
    stored_ref,
    scale_hbm,
    raw_ref,
    rows_ref,
    slot_ref,
    scale_ref,
    own,
    signs,
    picked,
    block_max,
    row_out,
    gathered,
    hub_out,
    hub_in,
    table_out,
    table,
    own_sem,
    small_sem,
    near_sem,
    right_sem,
    left_sem,
    in_sem,
    gather_sem,
    hub_sem,
    row_sem,
    pass_sem,
    send_near,
    send_right,
    send_left,
    send_in,
    send_gather,
    send_hub,
    send_row,
    send_pass,
    ready,
    *held_refs,
):
    held = [held_refs[k * STAGES : (k + 1) * STAGES] for k in range(HOLD)]
    me = lax.axis_index("ep")
    tp = lax.axis_index("tp")
    here_y, here_x = me // NX, lax.rem(me, NX)
    row_blocks = stored_ref.shape[0] // BLOCK
    is_hub = here_x == HUB

    def device(dy, x):
        return lax.rem(here_y + (NY + dy), NY) * NX + x, tp

    def across(dx):
        return lax.rem(here_x + dx, NX)

    barrier = pltpu.get_barrier_semaphore()
    for dy in range(-OUT, OUT + 1):
        for x in range(NX):
            if x == HUB:
                continue

            def greet(dy=dy, x=x):
                pl.semaphore_signal(barrier, inc=1, device_id=device(dy, x), device_id_type=MESH)

            if dy == 0:
                pl.when(here_x != x)(greet)
            else:
                greet()

    own_copy = pltpu.make_async_copy(stored_ref, own, own_sem)
    own_copy.start()
    slot_copy = pltpu.make_async_copy(slot_hbm, slot_ref, small_sem.at[0])
    slot_copy.start()
    scale_copy = pltpu.make_async_copy(scale_hbm, scale_ref, small_sem.at[1])
    scale_copy.start()

    @pl.when(is_hub)
    def _():
        def greet(step, _):
            pl.semaphore_signal(
                barrier, inc=1, device_id=(me, lax.rem(tp + step, tp_size)), device_id_type=MESH
            )
            return _

        lax.fori_loop(1, tp_size, greet, 0)

    @pl.when(jnp.logical_not(is_hub))
    def _():
        pl.semaphore_wait(barrier, (2 * OUT + 1) * NX - 1)

    @pl.when(here_x == HUB + 1)
    def _():
        pl.semaphore_signal(ready, inc=1, device_id=device(0, HUB), device_id_type=MESH)

    @pl.when(is_hub)
    def _():
        pl.semaphore_wait(ready, 1)

    def near_copy(rel, dx, stage, local=False):
        k = min(max(rel, 0), LAST)
        dy = k - rel
        chunk = lax.rem(here_y + (2 * NY - rel), NY)
        to_x = across(dx)
        start = pl.multiple_of((chunk * NX + to_x) * BLOCK + stage * PIECE, PIECE)
        source = stored_ref.at[pl.ds(start, PIECE)]
        target = held[k][stage].at[(rel + OUT) * NX + here_x]
        if local:
            return pltpu.make_async_copy(source, target, near_sem.at[k, stage])
        return pltpu.make_async_remote_copy(
            src_ref=source,
            dst_ref=target,
            send_sem=send_near,
            recv_sem=near_sem.at[k, stage],
            device_id=device(dy, to_x),
            device_id_type=MESH,
        )

    outside = [rel for reach in range(OUT, 0, -1) for rel in (-reach, LAST + reach)]
    inside = list(range(HOLD))
    for stage in range(STAGES):

        def send_outside(dx, _, stage=stage):
            for rel in outside:
                near_copy(rel, dx, stage).start()
            return _

        def send_inside(dx, _, stage=stage):
            for rel in inside:
                near_copy(rel, dx, stage).start()
            return _

        lax.fori_loop(0, NX, send_outside, 0)
        lax.fori_loop(1, NX, send_inside, 0)
        for rel in inside:
            near_copy(rel, 0, stage, local=True).start()

    signs[...] = sign_matrix()
    own_copy.wait()
    slot_copy.wait()
    scale_copy.wait()

    def some_blocks(index, _):
        at = pl.multiple_of(index * 8, 8)
        rows = own[pl.ds(pl.multiple_of(at * BLOCK, 8 * BLOCK), 8 * BLOCK), :]
        turned = jnp.dot(rows, signs[...], preferred_element_type=jnp.float32)
        block_max[pl.ds(at, 8), :] = jnp.max(jnp.abs(turned).reshape(8, BLOCK, BLOCK), axis=1)
        return _

    lax.fori_loop(0, row_blocks // 8, some_blocks, 0)
    row_out[...] = jnp.zeros_like(row_out)
    row_out[0, :, 0:row_blocks] = scale_ref[...].astype(jnp.float32)
    scale_row = row_out[0, :, :]
    largest = jnp.max(block_max[...] * to_column(scale_row, row_blocks)) * (1.0 / math.sqrt(BLOCK))
    lane = lax.broadcasted_iota(jnp.int32, (1, BLOCK), 1)
    row_out[0, :, :] = jnp.where(lane < row_blocks, scale_row, largest)

    gather_copy = pltpu.make_async_remote_copy(
        src_ref=row_out.at[0],
        dst_ref=gathered.at[here_x],
        send_sem=send_gather,
        recv_sem=gather_sem,
        device_id=device(0, HUB),
        device_id_type=MESH,
    )

    @pl.when(is_hub)
    def _():
        pltpu.make_async_copy(row_out.at[0], gathered.at[here_x], gather_sem).start()

    @pl.when(jnp.logical_not(is_hub))
    def _():
        gather_copy.start()

    lane3 = lax.broadcasted_iota(jnp.int32, (NX, 1, BLOCK), 2)

    def meet_hubs():
        @pl.when(is_hub)
        def _():
            pl.semaphore_wait(barrier, tp_size - 1)
            pltpu.make_async_copy(gathered, gathered, gather_sem).wait()
            hub_out[...] = gathered[...]

            def send_hub_row(step, _):
                pltpu.make_async_remote_copy(
                    src_ref=hub_out,
                    dst_ref=hub_in.at[tp],
                    send_sem=send_hub,
                    recv_sem=hub_sem,
                    device_id=(me, lax.rem(tp + step, tp_size)),
                    device_id_type=MESH,
                ).start()
                return _

            lax.fori_loop(1, tp_size, send_hub_row, 0)
            pltpu.make_async_copy(hub_out, hub_in.at[tp], hub_sem).start()

    def own_rows(dy):
        return table.at[pl.ds(lax.rem(here_y + (NY + dy), NY) * NX, NX)]

    def spread_rows():
        @pl.when(is_hub)
        def _():
            pltpu.make_async_copy(hub_in, hub_in, hub_sem).wait()
            table_out[...] = jnp.where(lane3 < row_blocks, hub_out[...], jnp.max(hub_in[...], axis=0))
            pltpu.make_async_copy(table_out, own_rows(0), row_sem).start()
            for dy in range(-OUT, OUT + 1):

                def send_rows(dx, _, dy=dy):
                    pltpu.make_async_remote_copy(
                        src_ref=table_out,
                        dst_ref=own_rows(0),
                        send_sem=send_row.at[dy + OUT],
                        recv_sem=row_sem,
                        device_id=device(dy, across(dx)),
                        device_id_type=MESH,
                    ).start()
                    return _

                lax.fori_loop(1 if dy == 0 else 0, NX, send_rows, 0)

    passed = [(-OUT, step) for step in range(1, NY // 2 - OUT + 1)]
    passed += [(OUT, -step) for step in range(1, (NY - 1) // 2 - OUT + 1)]

    def pass_copy(dy, step):
        return pltpu.make_async_remote_copy(
            src_ref=own_rows(step),
            dst_ref=own_rows(step),
            send_sem=send_pass,
            recv_sem=pass_sem,
            device_id=device(dy, here_x),
            device_id_type=MESH,
        )

    def pass_rows():
        near = table.at[pl.ds(0, (2 * OUT + 1) * NX)]
        pltpu.make_async_copy(near, near, row_sem).wait()
        for dy, step in passed:
            pass_copy(dy, step).start()

    def right_copy(k, stage):
        part = pl.ds(0, (OUT + k + 1) * NX)
        return pltpu.make_async_remote_copy(
            src_ref=held[k][stage].at[part],
            dst_ref=held[k + 1][stage].at[part],
            send_sem=send_right.at[k, stage],
            recv_sem=right_sem.at[k + 1, stage],
            device_id=device(1, here_x),
            device_id_type=MESH,
        )

    def left_copy(k, stage):
        part = pl.ds((OUT + k) * NX, (NY - OUT - k) * NX)
        return pltpu.make_async_remote_copy(
            src_ref=held[k][stage].at[part],
            dst_ref=held[k - 1][stage].at[part],
            send_sem=send_left.at[k, stage],
            recv_sem=left_sem.at[k - 1, stage],
            device_id=device(-1, here_x),
            device_id_type=MESH,
        )

    waited = set()

    def wait_near(k, stage):
        if (k, stage) not in waited:
            waited.add((k, stage))
            rows = NX * (OUT + 1 if k in (0, LAST) else 1)
            part = held[k][stage].at[pl.ds(0, rows)]
            pltpu.make_async_copy(part, part, near_sem.at[k, stage]).wait()

    def relay(level, stage):
        k = level
        wait_near(k, stage)
        if level > 0:
            right_copy(k - 1, stage).wait_recv()
        right_copy(k, stage).start()
        k = LAST - level
        wait_near(k, stage)
        if level > 0:
            left_copy(k + 1, stage).wait_recv()
        left_copy(k, stage).start()

    serves = [pair for reach in range(OUT, 0, -1) for pair in ((0, -reach), (LAST, reach))]
    far_count = len(serves)
    serves += [(k, 0) for k in range(HOLD)]

    def in_rows(k, stage):
        chunk = lax.rem(here_y + NY - k, NY)
        start = pl.multiple_of((chunk * NX + here_x) * BLOCK + stage * PIECE, PIECE)
        return raw_ref.at[:, pl.ds(start, PIECE)]

    def serve(stage):
        right_copy(LAST - 1, stage).wait_recv()
        left_copy(1, stage).wait_recv()

        def pick(dx, _):
            for at, (k, dy) in enumerate(serves):
                target, _tp = device(dy, across(dx))
                for slot in range(2):
                    expert = slot_ref[2 * target + slot]
                    away = ((expert >> 2) + (NY + k + OUT) - here_y) & 7
                    index = away * NX + (expert & 3)
                    picked[stage, at * NX + dx, slot] = held[k][stage][index]
            return _

        lax.fori_loop(0, NX, pick, 0)

        def send_in_one(dx, _, pairs):
            for at, (k, dy) in pairs:
                pltpu.make_async_remote_copy(
                    src_ref=picked.at[stage, at * NX + dx],
                    dst_ref=in_rows(k, stage),
                    send_sem=send_in,
                    recv_sem=in_sem.at[stage],
                    device_id=device(dy, across(dx)),
                    device_id_type=MESH,
                ).start()
            return _

        pairs = list(enumerate(serves))
        lax.fori_loop(0, NX, functools.partial(send_in_one, pairs=pairs[:far_count]), 0)
        lax.fori_loop(1, NX, functools.partial(send_in_one, pairs=pairs[far_count:]), 0)
        for at, (k, _dy) in pairs[far_count:]:
            pltpu.make_async_copy(
                picked.at[stage, at * NX], in_rows(k, stage), in_sem.at[stage]
            ).start()

    for turn in range(STAGES + LAST):
        for level in range(LAST):
            if 0 <= turn - level < STAGES:
                relay(level, turn - level)
        if turn == 1:
            meet_hubs()
        if turn == LAST:
            spread_rows()
        if turn == STAGES + LAST - 1:
            pass_rows()
        if turn >= LAST:
            serve(turn - LAST)

    passing = table.at[pl.ds(0, len(passed) * NX)]
    pltpu.make_async_copy(passing, passing, pass_sem).wait()
    for slot in range(2):
        rows_ref[slot] = table[slot_ref[2 * me + slot]]
    for stage in range(STAGES):
        part = raw_ref.at[:, pl.ds(0, EP * PIECE)]
        pltpu.make_async_copy(part, part, in_sem.at[stage]).wait()
    remote = EP - HOLD
    sent = own.at[pl.ds(0, remote * BLOCK)]
    pltpu.make_async_copy(sent, sent, send_near).wait()
    for stage in range(STAGES):
        for level in range(LAST):
            right_copy(level, stage).wait_send()
            left_copy(LAST - level, stage).wait_send()
    sent = picked.at[:, pl.ds(0, remote)]
    pltpu.make_async_copy(sent, sent, send_in).wait()
    pltpu.make_async_copy(passing, passing, send_pass).wait()

    @pl.when(jnp.logical_not(is_hub))
    def _():
        gather_copy.wait_send()

    @pl.when(is_hub)
    def _():
        sent = hub_in.at[pl.ds(0, tp_size - 1)]
        pltpu.make_async_copy(sent, sent, send_hub).wait()
        for dy in range(-OUT, OUT + 1):
            sent = hub_in.at[pl.ds(0, NX - 1 if dy == 0 else NX)]
            pltpu.make_async_copy(sent, sent, send_row.at[dy + OUT]).wait()


def move_rows(tp_size, stored, scale, slot_expert):
    rows = stored.shape[0]
    row_blocks = rows // BLOCK
    dma = pltpu.SemaphoreType.DMA
    return pl.pallas_call(
        functools.partial(move_kernel, tp_size),
        out_shape=(
            jax.ShapeDtypeStruct((2, rows, BLOCK), jnp.bfloat16),
            jax.ShapeDtypeStruct((2, 1, BLOCK), jnp.float32),
        ),
        in_specs=[pl.BlockSpec(memory_space=pltpu.HBM)] * 3,
        out_specs=(
            pl.BlockSpec(memory_space=pl.ANY),
            pl.BlockSpec(memory_space=pltpu.VMEM),
        ),
        scratch_shapes=[
            pltpu.SMEM(slot_expert.shape, jnp.int32),
            pltpu.VMEM(scale.shape, jnp.bfloat16),
            pltpu.VMEM((rows, BLOCK), jnp.bfloat16),
            pltpu.VMEM((BLOCK, BLOCK), jnp.bfloat16),
            pltpu.VMEM((STAGES, EP, 2, PIECE, BLOCK), jnp.bfloat16),
            pltpu.VMEM((row_blocks, BLOCK), jnp.float32),
            pltpu.VMEM((1, 1, BLOCK), jnp.float32),
            pltpu.VMEM((NX, 1, BLOCK), jnp.float32),
            pltpu.VMEM((NX, 1, BLOCK), jnp.float32),
            pltpu.VMEM((tp_size, NX, 1, BLOCK), jnp.float32),
            pltpu.VMEM((NX, 1, BLOCK), jnp.float32),
            pltpu.VMEM((EP, 1, BLOCK), jnp.float32),
            dma,
            dma((2,)),
            dma((HOLD, STAGES)),
            dma((HOLD, STAGES)),
            dma((HOLD, STAGES)),
            dma((STAGES,)),
            dma,
            dma,
            dma,
            dma,
            dma,
            dma((HOLD, STAGES)),
            dma((HOLD, STAGES)),
            dma,
            dma,
            dma,
            dma((2 * OUT + 1,)),
            dma,
            pltpu.SemaphoreType.REGULAR,
        ]
        + [pltpu.VMEM((EP, PIECE, BLOCK), jnp.bfloat16)] * (HOLD * STAGES),
        compiler_params=pltpu.CompilerParams(
            collective_id=0, has_side_effects=True, vmem_limit_bytes=VMEM_LIMIT
        ),
        name="move_rows",
    )(*(pltpu.with_memory_space_constraint(a, pltpu.HBM) for a in (slot_expert, stored, scale)))


TILE = 1024


def finish_kernel(raw_ref, rows_ref, out_ref, largest_ref, staged, factors, sems):
    count, rows, _ = staged.shape
    row_blocks = rows // BLOCK
    blocks = TILE // BLOCK
    signs = sign_matrix()
    lane = lax.broadcasted_iota(jnp.int32, (1, BLOCK), 1)
    copies = []
    for slot in range(count):
        row = rows_ref[slot]
        largest = jnp.max(jnp.where(lane < row_blocks, 0.0, row))
        largest_ref[slot] = largest
        bound = jnp.full((row_blocks, BLOCK), largest, jnp.float32) + EPSILON
        scale = jnp.broadcast_to(to_column(row, row_blocks), (row_blocks, BLOCK))
        factors[slot] = (scale * (1.0 / math.sqrt(BLOCK))) / bound
        for tile in range(rows // TILE):
            at = pl.ds(tile * TILE, TILE)
            turned = jnp.dot(raw_ref[slot, at, :], signs, preferred_element_type=jnp.float32)
            factor = factors[slot, pl.ds(tile * blocks, blocks), :]
            scaled = turned.reshape(blocks, BLOCK, BLOCK) * factor[:, None, :]
            staged[slot, at, :] = scaled.reshape(TILE, BLOCK).astype(jnp.bfloat16)
            copy = pltpu.make_async_copy(
                staged.at[slot, at], out_ref.at[slot, at], sems.at[slot, tile]
            )
            copy.start()
            copies.append(copy)
    for copy in copies:
        copy.wait()


def finish(raw, rows):
    count, height, width = raw.shape
    return pl.pallas_call(
        finish_kernel,
        out_shape=(
            jax.ShapeDtypeStruct(raw.shape, jnp.bfloat16),
            jax.ShapeDtypeStruct((count,), jnp.float32),
        ),
        in_specs=[
            pl.BlockSpec(memory_space=pltpu.VMEM),
            pl.BlockSpec(memory_space=pltpu.VMEM),
        ],
        out_specs=(
            pl.BlockSpec(memory_space=pltpu.HBM),
            pl.BlockSpec(memory_space=pltpu.SMEM),
        ),
        scratch_shapes=[
            pltpu.VMEM(raw.shape, jnp.bfloat16),
            pltpu.VMEM((count, height // BLOCK, BLOCK), jnp.float32),
            pltpu.SemaphoreType.DMA((count, height // TILE)),
        ],
        compiler_params=pltpu.CompilerParams(vmem_limit_bytes=VMEM_LIMIT),
        name="finish",
    )(raw, rows)


def on_device(tp_size, quantized, block_scale, slot_expert):
    rows = quantized.shape[1]
    stored = quantized.reshape(rows, BLOCK)
    scale = block_scale.reshape(1, rows // BLOCK)
    raw, picked_rows = move_rows(tp_size, stored, scale, slot_expert)
    return finish(raw, picked_rows)


def solution(mesh):
    in_specs = (P("ep", None, "tp"), P("ep", None, "tp"), P())
    out_specs = (P("ep", None, "tp"), P("ep"))
    return jax.shard_map(
        functools.partial(on_device, mesh.shape["tp"]),
        mesh=mesh,
        in_specs=in_specs,
        out_specs=out_specs,
        check_vma=False,
    )
```

time: 184 us -> 74.6 us (0.41)
  waiting for transfers between devices: 77.2 us -> 0 us
  Pallas kernels: 0 us -> 73.8 us
  starting transfers between devices: 31.1 us -> 0 us
  blocking collectives: 30.1 us -> 0 us
  other arithmetic: 29 us -> 0 us
  local copies, waits for them, and re-layouts: 9.89 us -> 0 us
  matrix products: 5.1 us -> 0 us
    all_to_all x4 -> x0, waiting for transfers between devices: 77.2 us -> none  [the longest x1 47.1 us: on_device(): lax.all_to_all(picked_vals, 'ep', split_axis=0, concat_axis=1, tiled=True)]
    pallas_call x0 -> x2, Pallas kernels: none -> 73.8 us  [the longest x1 71.6 us: move_rows(): pl.pallas_call(functools.partial(move_kernel, tp_size), out_shape=(jax.Sh...]
    all_to_all x4 -> x0, starting transfers between devices: 31.1 us -> none  [the longest x1 10.2 us: on_device(): lax.all_to_all(block_scale, 'ep', split_axis=1, concat_axis=0, tiled=True)]
    pmax x1 -> x0, blocking collectives: 30.1 us -> none  [on_device(): largest = lax.pmax(local_max, 'tp')]
    unnamed x1 -> x0, other arithmetic: 22.4 us -> none
    unnamed x10 -> x0, local copies, waits for them, and re-layouts: 7.34 us -> none
    dot_general x1 -> x0, matrix products: 5.1 us -> none  [rotate_blocks(): jnp.einsum('eiajb,bc->eiajc', blocks, hadamard(BLOCK), precision=lax.Prec...]
    convert_element_type x2 -> x0, other arithmetic: 4.68 us -> none  [the longest x1 4.12 us: normalize(): scaled.reshape(count, row_blocks * width_a, col_blocks * width_b)]
  transfers between devices with their start and end apart: 4 -> 0, of which waited for: 3 -> 0; matrix products, arithmetic and copies ran while one was open for 18% -> 0% of each run, Pallas kernels for 0% -> 0%
where the time goes in v2:
time: 74.6 us; the launch traced here: 74.4 us
  Pallas kernels  73.8 us (99%)
    pallas_call x1, Pallas kernels, move_rows(): pl.pallas_call(functools.partial(move_kernel, tp_size), out_shape=(jax.Sh...  71.6 us
    pallas_call x1, Pallas kernels, finish(): pl.pallas_call(finish_kernel, out_shape=(jax.ShapeDtypeStruct(raw.shape,...  2.24 us

profile of v2, /device:TPU:6, one launch (start us, length us, event | category | flops | bytes accessed | tf_op | source)
XLA Modules:
  0.0 74.4 jit_solution(11056108167938655241)
XLA Ops:
  0.6 71.6 %move_rows.1 = (bf16[2,4096,128]{2,1,0:T(8,128)(2,1)S(1)}, f32[2,1,128]{2,1,0:T(1,128)S(1)}) custom-call(s32[64]{0:T(128)} %slot_hbm.1, bf16[4096,128]{1,0:T(8,128)(2,1)} %bitcast.2, bf16[1,32]{1,0:T(2,128)(2,1)} %bitcast.3), custom_call_target="tpu_custom_call" | custom-call | tf_op jit(solution)/shard_map/move_rows/pallas_call | solution.py:415
  72.2 2.2 %finish.1 = (bf16[2,4096,128]{2,1,0:T(8,128)(2,1)}, f32[2]{0:T(128)}) custom-call(bf16[2,4096,128]{2,1,0:T(8,128)(2,1)S(1)} %get-tuple-element.4.raw_ref, f32[2,1,128]{2,1,0:T(1,128)S(1)} %get-tuple-element.5.rows_ref), custom_call_target="tpu_custom_call" | custom-call | tf_op jit(solution)/shard_map/finish/pallas_call | solution.py:501

commit v3 on v2

--- a/solution.py
+++ b/solution.py
@@ -16,8 +16,11 @@
 HOLD = 4
 OUT = (NY - HOLD) // 2
 LAST = HOLD - 1
-STAGES = 4
-PIECE = BLOCK // STAGES
+PIECES = (32, 32, 32, 32)
+SUBS = (1, 1, 1, 1)
+STAGES = len(PIECES)
+STEPS = tuple((stage, part) for stage in range(len(PIECES)) for part in range(SUBS[stage]))
+STARTS = tuple(sum(PIECES[:stage]) for stage in range(STAGES))
 HUB = 0
 VMEM_LIMIT = 16 << 20
 
@@ -50,7 +53,6 @@
     scale_ref,
     own,
     signs,
-    picked,
     block_max,
     row_out,
     gathered,
@@ -77,9 +79,10 @@
     send_row,
     send_pass,
     ready,
-    *held_refs,
+    *buffers,
 ):
-    held = [held_refs[k * STAGES : (k + 1) * STAGES] for k in range(HOLD)]
+    held = [buffers[k * STAGES : (k + 1) * STAGES] for k in range(HOLD)]
+    picked = buffers[HOLD * STAGES :]
     me = lax.axis_index("ep")
     tp = lax.axis_index("tp")
     here_y, here_x = me // NX, lax.rem(me, NX)
@@ -140,8 +143,8 @@
         dy = k - rel
         chunk = lax.rem(here_y + (2 * NY - rel), NY)
         to_x = across(dx)
-        start = pl.multiple_of((chunk * NX + to_x) * BLOCK + stage * PIECE, PIECE)
-        source = stored_ref.at[pl.ds(start, PIECE)]
+        start = pl.multiple_of((chunk * NX + to_x) * BLOCK + STARTS[stage], 16)
+        source = stored_ref.at[pl.ds(start, PIECES[stage])]
         target = held[k][stage].at[(rel + OUT) * NX + here_x]
         if local:
             return pltpu.make_async_copy(source, target, near_sem.at[k, stage])
@@ -156,42 +159,23 @@
 
     outside = [rel for reach in range(OUT, 0, -1) for rel in (-reach, LAST + reach)]
     inside = list(range(HOLD))
-    for stage in range(STAGES):
-
-        def send_outside(dx, _, stage=stage):
-            for rel in outside:
+
+    def send_near_to(rels, stage):
+        def send(dx, _):
+            for rel in rels:
                 near_copy(rel, dx, stage).start()
             return _
 
-        def send_inside(dx, _, stage=stage):
-            for rel in inside:
-                near_copy(rel, dx, stage).start()
-            return _
-
-        lax.fori_loop(0, NX, send_outside, 0)
-        lax.fori_loop(1, NX, send_inside, 0)
+        lax.fori_loop(1 if rels[0] in inside else 0, NX, send, 0)
+
+    for stage in range(STAGES):
+        send_near_to(outside, stage)
+        send_near_to([0, LAST], stage)
         for rel in inside:
             near_copy(rel, 0, stage, local=True).start()
-
-    signs[...] = sign_matrix()
-    own_copy.wait()
-    slot_copy.wait()
-    scale_copy.wait()
-
-    def some_blocks(index, _):
-        at = pl.multiple_of(index * 8, 8)
-        rows = own[pl.ds(pl.multiple_of(at * BLOCK, 8 * BLOCK), 8 * BLOCK), :]
-        turned = jnp.dot(rows, signs[...], preferred_element_type=jnp.float32)
-        block_max[pl.ds(at, 8), :] = jnp.max(jnp.abs(turned).reshape(8, BLOCK, BLOCK), axis=1)
-        return _
-
-    lax.fori_loop(0, row_blocks // 8, some_blocks, 0)
-    row_out[...] = jnp.zeros_like(row_out)
-    row_out[0, :, 0:row_blocks] = scale_ref[...].astype(jnp.float32)
-    scale_row = row_out[0, :, :]
-    largest = jnp.max(block_max[...] * to_column(scale_row, row_blocks)) * (1.0 / math.sqrt(BLOCK))
-    lane = lax.broadcasted_iota(jnp.int32, (1, BLOCK), 1)
-    row_out[0, :, :] = jnp.where(lane < row_blocks, scale_row, largest)
+        if stage > 0:
+            send_near_to(inside[1:-1], stage - 1)
+    send_near_to(inside[1:-1], STAGES - 1)
 
     gather_copy = pltpu.make_async_remote_copy(
         src_ref=row_out.at[0],
@@ -202,13 +186,34 @@
         device_id_type=MESH,
     )
 
-    @pl.when(is_hub)
-    def _():
-        pltpu.make_async_copy(row_out.at[0], gathered.at[here_x], gather_sem).start()
-
-    @pl.when(jnp.logical_not(is_hub))
-    def _():
-        gather_copy.start()
+    def find_largest():
+        signs[...] = sign_matrix()
+        own_copy.wait()
+        slot_copy.wait()
+        scale_copy.wait()
+
+        def some_blocks(index, _):
+            at = pl.multiple_of(index * 8, 8)
+            rows = own[pl.ds(pl.multiple_of(at * BLOCK, 8 * BLOCK), 8 * BLOCK), :]
+            turned = jnp.dot(rows, signs[...], preferred_element_type=jnp.float32)
+            block_max[pl.ds(at, 8), :] = jnp.max(jnp.abs(turned).reshape(8, BLOCK, BLOCK), axis=1)
+            return _
+
+        lax.fori_loop(0, row_blocks // 8, some_blocks, 0)
+        row_out[...] = jnp.zeros_like(row_out)
+        row_out[0, :, 0:row_blocks] = scale_ref[...].astype(jnp.float32)
+        scale_row = row_out[0, :, :]
+        largest = jnp.max(block_max[...] * to_column(scale_row, row_blocks)) * (1.0 / math.sqrt(BLOCK))
+        lane = lax.broadcasted_iota(jnp.int32, (1, BLOCK), 1)
+        row_out[0, :, :] = jnp.where(lane < row_blocks, scale_row, largest)
+
+        @pl.when(is_hub)
+        def _():
+            pltpu.make_async_copy(row_out.at[0], gathered.at[here_x], gather_sem).start()
+
+        @pl.when(jnp.logical_not(is_hub))
+        def _():
+            gather_copy.start()
 
     lane3 = lax.broadcasted_iota(jnp.int32, (NX, 1, BLOCK), 2)
 
@@ -276,48 +281,54 @@
         for dy, step in passed:
             pass_copy(dy, step).start()
 
-    def right_copy(k, stage):
-        part = pl.ds(0, (OUT + k + 1) * NX)
+    def relay_part(k, step, experts):
+        stage, part = STEPS[step]
+        height = PIECES[stage] // SUBS[stage]
+        return held[k][stage].at[experts, pl.ds(part * height, height)]
+
+    def right_copy(k, step):
+        experts = pl.ds(0, (OUT + k + 1) * NX)
         return pltpu.make_async_remote_copy(
-            src_ref=held[k][stage].at[part],
-            dst_ref=held[k + 1][stage].at[part],
-            send_sem=send_right.at[k, stage],
-            recv_sem=right_sem.at[k + 1, stage],
+            src_ref=relay_part(k, step, experts),
+            dst_ref=relay_part(k + 1, step, experts),
+            send_sem=send_right.at[k, step],
+            recv_sem=right_sem.at[k + 1, step],
             device_id=device(1, here_x),
             device_id_type=MESH,
         )
 
-    def left_copy(k, stage):
-        part = pl.ds((OUT + k) * NX, (NY - OUT - k) * NX)
+    def left_copy(k, step):
+        experts = pl.ds((OUT + k) * NX, (NY - OUT - k) * NX)
         return pltpu.make_async_remote_copy(
-            src_ref=held[k][stage].at[part],
-            dst_ref=held[k - 1][stage].at[part],
-            send_sem=send_left.at[k, stage],
-            recv_sem=left_sem.at[k - 1, stage],
+            src_ref=relay_part(k, step, experts),
+            dst_ref=relay_part(k - 1, step, experts),
+            send_sem=send_left.at[k, step],
+            recv_sem=left_sem.at[k - 1, step],
             device_id=device(-1, here_x),
             device_id_type=MESH,
         )
 
     waited = set()
 
-    def wait_near(k, stage):
+    def wait_near(k, step):
+        stage = STEPS[step][0]
         if (k, stage) not in waited:
             waited.add((k, stage))
             rows = NX * (OUT + 1 if k in (0, LAST) else 1)
             part = held[k][stage].at[pl.ds(0, rows)]
             pltpu.make_async_copy(part, part, near_sem.at[k, stage]).wait()
 
-    def relay(level, stage):
+    def relay(level, step):
         k = level
-        wait_near(k, stage)
+        wait_near(k, step)
         if level > 0:
-            right_copy(k - 1, stage).wait_recv()
-        right_copy(k, stage).start()
+            right_copy(k - 1, step).wait_recv()
+        right_copy(k, step).start()
         k = LAST - level
-        wait_near(k, stage)
+        wait_near(k, step)
         if level > 0:
-            left_copy(k + 1, stage).wait_recv()
-        left_copy(k, stage).start()
+            left_copy(k + 1, step).wait_recv()
+        left_copy(k, step).start()
 
     serves = [pair for reach in range(OUT, 0, -1) for pair in ((0, -reach), (LAST, reach))]
     far_count = len(serves)
@@ -325,31 +336,27 @@
 
     def in_rows(k, stage):
         chunk = lax.rem(here_y + NY - k, NY)
-        start = pl.multiple_of((chunk * NX + here_x) * BLOCK + stage * PIECE, PIECE)
-        return raw_ref.at[:, pl.ds(start, PIECE)]
-
-    def serve(stage):
-        right_copy(LAST - 1, stage).wait_recv()
-        left_copy(1, stage).wait_recv()
-
-        def pick(dx, _):
-            for at, (k, dy) in enumerate(serves):
+        start = pl.multiple_of((chunk * NX + here_x) * BLOCK + STARTS[stage], 16)
+        return raw_ref.at[:, pl.ds(start, PIECES[stage])]
+
+    def serve(stage, part):
+        def pick(dx, _, pairs):
+            for at, (k, dy) in pairs:
                 target, _tp = device(dy, across(dx))
                 for slot in range(2):
                     expert = slot_ref[2 * target + slot]
                     away = ((expert >> 2) + (NY + k + OUT) - here_y) & 7
                     index = away * NX + (expert & 3)
-                    picked[stage, at * NX + dx, slot] = held[k][stage][index]
+                    picked[stage][at * NX + dx, slot] = held[k][stage][index]
             return _
 
-        lax.fori_loop(0, NX, pick, 0)
-
-        def send_in_one(dx, _, pairs):
+        def send_in_one(turn, _, pairs):
+            dx = lax.rem(2 + 3 * turn, NX) if pairs[0][0] < far_count else turn
             for at, (k, dy) in pairs:
                 pltpu.make_async_remote_copy(
-                    src_ref=picked.at[stage, at * NX + dx],
+                    src_ref=picked[stage].at[at * NX + dx],
                     dst_ref=in_rows(k, stage),
-                    send_sem=send_in,
+                    send_sem=send_in.at[stage],
                     recv_sem=in_sem.at[stage],
                     device_id=device(dy, across(dx)),
                     device_id_type=MESH,
@@ -357,42 +364,66 @@
             return _
 
         pairs = list(enumerate(serves))
-        lax.fori_loop(0, NX, functools.partial(send_in_one, pairs=pairs[:far_count]), 0)
-        lax.fori_loop(1, NX, functools.partial(send_in_one, pairs=pairs[far_count:]), 0)
+        far, rest = pairs[:far_count], pairs[far_count:]
+        far, rest = ((far + rest, rest), (far[:2], []), (far[2:] + rest, rest))[part]
+        far = [pair for pair in far if pair not in rest]
+        lax.fori_loop(0, NX, functools.partial(pick, pairs=far), 0)
+        for first in range(0, len(far), 2):
+            lax.fori_loop(0, NX, functools.partial(send_in_one, pairs=far[first : first + 2]), 0)
+        if not rest:
+            return
+        lax.fori_loop(0, NX, functools.partial(pick, pairs=rest), 0)
+        lax.fori_loop(1, NX, functools.partial(send_in_one, pairs=rest), 0)
         for at, (k, _dy) in pairs[far_count:]:
             pltpu.make_async_copy(
-                picked.at[stage, at * NX], in_rows(k, stage), in_sem.at[stage]
+                picked[stage].at[at * NX], in_rows(k, stage), in_sem.at[stage]
             ).start()
 
-    for turn in range(STAGES + LAST):
+    count = len(STEPS)
+    held_back = []
+    for turn in range(count + LAST):
         for level in range(LAST):
-            if 0 <= turn - level < STAGES:
+            if 0 <= turn - level < count:
                 relay(level, turn - level)
-        if turn == 1:
+        if turn == 0:
+            find_largest()
+        if turn == 2:
             meet_hubs()
-        if turn == LAST:
+        if turn == 4:
             spread_rows()
-        if turn == STAGES + LAST - 1:
+        if turn == count + LAST - 1:
             pass_rows()
+        while held_back:
+            serve(held_back.pop(), 2)
         if turn >= LAST:
-            serve(turn - LAST)
+            step = turn - LAST
+            right_copy(LAST - 1, step).wait_recv()
+            left_copy(1, step).wait_recv()
+            stage, part = STEPS[step]
+            if part == SUBS[stage] - 1:
+                if stage < STAGES - 1:
+                    serve(stage, 1)
+                    held_back.append(stage)
+                else:
+                    serve(stage, 0)
 
     passing = table.at[pl.ds(0, len(passed) * NX)]
     pltpu.make_async_copy(passing, passing, pass_sem).wait()
     for slot in range(2):
         rows_ref[slot] = table[slot_ref[2 * me + slot]]
     for stage in range(STAGES):
-        part = raw_ref.at[:, pl.ds(0, EP * PIECE)]
+        part = raw_ref.at[:, pl.ds(0, EP * PIECES[stage])]
         pltpu.make_async_copy(part, part, in_sem.at[stage]).wait()
     remote = EP - HOLD
     sent = own.at[pl.ds(0, remote * BLOCK)]
     pltpu.make_async_copy(sent, sent, send_near).wait()
+    for step in range(count):
+        for level in range(LAST):
+            right_copy(level, step).wait_send()
+            left_copy(LAST - level, step).wait_send()
     for stage in range(STAGES):
-        for level in range(LAST):
-            right_copy(level, stage).wait_send()
-            left_copy(LAST - level, stage).wait_send()
-    sent = picked.at[:, pl.ds(0, remote)]
-    pltpu.make_async_copy(sent, sent, send_in).wait()
+        sent = picked[stage].at[pl.ds(0, remote)]
+        pltpu.make_async_copy(sent, sent, send_in.at[stage]).wait()
     pltpu.make_async_copy(passing, passing, send_pass).wait()
 
     @pl.when(jnp.logical_not(is_hub))
@@ -428,7 +459,6 @@
             pltpu.VMEM(scale.shape, jnp.bfloat16),
             pltpu.VMEM((rows, BLOCK), jnp.bfloat16),
             pltpu.VMEM((BLOCK, BLOCK), jnp.bfloat16),
-            pltpu.VMEM((STAGES, EP, 2, PIECE, BLOCK), jnp.bfloat16),
             pltpu.VMEM((row_blocks, BLOCK), jnp.float32),
             pltpu.VMEM((1, 1, BLOCK), jnp.float32),
             pltpu.VMEM((NX, 1, BLOCK), jnp.float32),
@@ -439,24 +469,25 @@
             dma,
             dma((2,)),
             dma((HOLD, STAGES)),
-            dma((HOLD, STAGES)),
-            dma((HOLD, STAGES)),
+            dma((HOLD, len(STEPS))),
+            dma((HOLD, len(STEPS))),
             dma((STAGES,)),
             dma,
             dma,
             dma,
             dma,
             dma,
-            dma((HOLD, STAGES)),
-            dma((HOLD, STAGES)),
-            dma,
+            dma((HOLD, len(STEPS))),
+            dma((HOLD, len(STEPS))),
+            dma((STAGES,)),
             dma,
             dma,
             dma((2 * OUT + 1,)),
             dma,
             pltpu.SemaphoreType.REGULAR,
         ]
-        + [pltpu.VMEM((EP, PIECE, BLOCK), jnp.bfloat16)] * (HOLD * STAGES),
+        + [pltpu.VMEM((EP, piece, BLOCK), jnp.bfloat16) for piece in PIECES] * HOLD
+        + [pltpu.VMEM((EP, 2, piece, BLOCK), jnp.bfloat16) for piece in PIECES],
         compiler_params=pltpu.CompilerParams(
             collective_id=0, has_side_effects=True, vmem_limit_bytes=VMEM_LIMIT
         ),

time: 74.6 us -> 73.3 us (0.983)
  Pallas kernels: 73.8 us -> 72.6 us
    pallas_call x1, Pallas kernels: 71.6 us -> 70.3 us  [move_rows(): pl.pallas_call(functools.partial(move_kernel, tp_size), out_shape=(jax.Sh...]
where the time goes in v3:
time: 73.3 us; the launch traced here: 73.2 us
  Pallas kernels  72.6 us (99%)
    pallas_call x1, Pallas kernels, move_rows(): pl.pallas_call(functools.partial(move_kernel, tp_size), out_shape=(jax.Sh...  70.3 us
    pallas_call x1, Pallas kernels, finish(): pl.pallas_call(finish_kernel, out_shape=(jax.ShapeDtypeStruct(raw.shape,...  2.24 us

profile of v3, /device:TPU:6, one launch (start us, length us, event | category | flops | bytes accessed | tf_op | source)
XLA Modules:
  0.0 73.2 jit_solution(2469150299302711420)
XLA Ops:
  0.6 70.3 %move_rows.1 = (bf16[2,4096,128]{2,1,0:T(8,128)(2,1)S(1)}, f32[2,1,128]{2,1,0:T(1,128)S(1)}) custom-call(s32[64]{0:T(128)} %slot_hbm.1, bf16[4096,128]{1,0:T(8,128)(2,1)} %bitcast.2, bf16[1,32]{1,0:T(2,128)(2,1)} %bitcast.3), custom_call_target="tpu_custom_call" | custom-call | tf_op jit(solution)/shard_map/move_rows/pallas_call | solution.py:446
  71.0 2.2 %finish.1 = (bf16[2,4096,128]{2,1,0:T(8,128)(2,1)}, f32[2]{0:T(128)}) custom-call(bf16[2,4096,128]{2,1,0:T(8,128)(2,1)S(1)} %get-tuple-element.4.raw_ref, f32[2,1,128]{2,1,0:T(1,128)S(1)} %get-tuple-element.5.rows_ref), custom_call_target="tpu_custom_call" | custom-call | tf_op jit(solution)/shard_map/finish/pallas_call | solution.py:532

commit v4 on v3

--- a/solution.py
+++ b/solution.py
@@ -22,6 +22,7 @@
 STEPS = tuple((stage, part) for stage in range(len(PIECES)) for part in range(SUBS[stage]))
 STARTS = tuple(sum(PIECES[:stage]) for stage in range(STAGES))
 HUB = 0
+HELPER = 1
 VMEM_LIMIT = 16 << 20
 
 
@@ -48,17 +49,20 @@
     stored_ref,
     scale_hbm,
     raw_ref,
-    rows_ref,
+    largest_ref,
+    factors_ref,
+    signs,
     slot_ref,
     scale_ref,
     own,
-    signs,
     block_max,
     row_out,
+    top_out,
     gathered,
     hub_out,
     hub_in,
-    table_out,
+    plane_out,
+    tops,
     table,
     own_sem,
     small_sem,
@@ -70,6 +74,10 @@
     hub_sem,
     row_sem,
     pass_sem,
+    scale_sem,
+    tops_sem,
+    send_scale,
+    send_top,
     send_near,
     send_right,
     send_left,
@@ -87,7 +95,7 @@
     tp = lax.axis_index("tp")
     here_y, here_x = me // NX, lax.rem(me, NX)
     row_blocks = stored_ref.shape[0] // BLOCK
-    is_hub = here_x == HUB
+    is_hub = me == HUB
 
     def device(dy, x):
         return lax.rem(here_y + (NY + dy), NY) * NX + x, tp
@@ -96,18 +104,16 @@
         return lax.rem(here_x + dx, NX)
 
     barrier = pltpu.get_barrier_semaphore()
+    hub_y = HUB // NX
     for dy in range(-OUT, OUT + 1):
-        for x in range(NX):
-            if x == HUB:
+        for dx in range(NX):
+            if dy == 0 and dx == 0:
                 continue
-
-            def greet(dy=dy, x=x):
-                pl.semaphore_signal(barrier, inc=1, device_id=device(dy, x), device_id_type=MESH)
-
-            if dy == 0:
-                pl.when(here_x != x)(greet)
-            else:
-                greet()
+            target, _tp = device(dy, across(dx))
+
+            @pl.when(jnp.logical_not(is_hub) & (target != HUB))
+            def _(target=target):
+                pl.semaphore_signal(barrier, inc=1, device_id=(target, tp), device_id_type=MESH)
 
     own_copy = pltpu.make_async_copy(stored_ref, own, own_sem)
     own_copy.start()
@@ -126,13 +132,23 @@
 
         lax.fori_loop(1, tp_size, greet, 0)
 
+        def greet_plane(step, _):
+            pl.semaphore_signal(
+                barrier, inc=1, device_id=(lax.rem(me + step, EP), tp), device_id_type=MESH
+            )
+            return _
+
+        lax.fori_loop(1, EP, greet_plane, 0)
+
     @pl.when(jnp.logical_not(is_hub))
     def _():
-        pl.semaphore_wait(barrier, (2 * OUT + 1) * NX - 1)
-
-    @pl.when(here_x == HUB + 1)
+        away = lax.rem(here_y - hub_y + NY, NY)
+        beyond = (away > OUT) & (away < NY - OUT)
+        pl.semaphore_wait(barrier, (2 * OUT + 1) * NX - 1 + jnp.where(beyond, 1, 0))
+
+    @pl.when(me == HELPER)
     def _():
-        pl.semaphore_signal(ready, inc=1, device_id=device(0, HUB), device_id_type=MESH)
+        pl.semaphore_signal(ready, inc=1, device_id=(HUB, tp), device_id_type=MESH)
 
     @pl.when(is_hub)
     def _():
@@ -178,13 +194,23 @@
     send_near_to(inside[1:-1], STAGES - 1)
 
     gather_copy = pltpu.make_async_remote_copy(
-        src_ref=row_out.at[0],
-        dst_ref=gathered.at[here_x],
+        src_ref=top_out.at[0],
+        dst_ref=gathered.at[me],
         send_sem=send_gather,
         recv_sem=gather_sem,
-        device_id=device(0, HUB),
+        device_id=(HUB, tp),
         device_id_type=MESH,
     )
+
+    def scale_copy_to(dx):
+        return pltpu.make_async_remote_copy(
+            src_ref=row_out.at[0],
+            dst_ref=table.at[me],
+            send_sem=send_scale,
+            recv_sem=scale_sem,
+            device_id=device(0, across(dx)),
+            device_id_type=MESH,
+        )
 
     def find_largest():
         signs[...] = sign_matrix()
@@ -204,29 +230,31 @@
         row_out[0, :, 0:row_blocks] = scale_ref[...].astype(jnp.float32)
         scale_row = row_out[0, :, :]
         largest = jnp.max(block_max[...] * to_column(scale_row, row_blocks)) * (1.0 / math.sqrt(BLOCK))
-        lane = lax.broadcasted_iota(jnp.int32, (1, BLOCK), 1)
-        row_out[0, :, :] = jnp.where(lane < row_blocks, scale_row, largest)
+        top_out[...] = jnp.full((1, 1, BLOCK), largest, jnp.float32)
+        pltpu.make_async_copy(row_out.at[0], table.at[me], scale_sem).start()
+        for dx in range(1, NX):
+            scale_copy_to(dx).start()
 
         @pl.when(is_hub)
         def _():
-            pltpu.make_async_copy(row_out.at[0], gathered.at[here_x], gather_sem).start()
+            pltpu.make_async_copy(top_out.at[0], gathered.at[me], gather_sem).start()
 
         @pl.when(jnp.logical_not(is_hub))
         def _():
             gather_copy.start()
-
-    lane3 = lax.broadcasted_iota(jnp.int32, (NX, 1, BLOCK), 2)
 
     def meet_hubs():
         @pl.when(is_hub)
         def _():
             pl.semaphore_wait(barrier, tp_size - 1)
             pltpu.make_async_copy(gathered, gathered, gather_sem).wait()
-            hub_out[...] = gathered[...]
+            experts = lax.broadcasted_iota(jnp.int32, (EP, 1, BLOCK), 0)
+            lanes = lax.broadcasted_iota(jnp.int32, (EP, 1, BLOCK), 2)
+            hub_out[0] = jnp.max(jnp.where(experts == lanes, gathered[...], 0.0), axis=0)
 
             def send_hub_row(step, _):
                 pltpu.make_async_remote_copy(
-                    src_ref=hub_out,
+                    src_ref=hub_out.at[0],
                     dst_ref=hub_in.at[tp],
                     send_sem=send_hub,
                     recv_sem=hub_sem,
@@ -236,31 +264,44 @@
                 return _
 
             lax.fori_loop(1, tp_size, send_hub_row, 0)
-            pltpu.make_async_copy(hub_out, hub_in.at[tp], hub_sem).start()
-
-    def own_rows(dy):
-        return table.at[pl.ds(lax.rem(here_y + (NY + dy), NY) * NX, NX)]
-
-    def spread_rows():
+            pltpu.make_async_copy(hub_out.at[0], hub_in.at[tp], hub_sem).start()
+
+    def spread_tops():
         @pl.when(is_hub)
         def _():
             pltpu.make_async_copy(hub_in, hub_in, hub_sem).wait()
-            table_out[...] = jnp.where(lane3 < row_blocks, hub_out[...], jnp.max(hub_in[...], axis=0))
-            pltpu.make_async_copy(table_out, own_rows(0), row_sem).start()
-            for dy in range(-OUT, OUT + 1):
-
-                def send_rows(dx, _, dy=dy):
-                    pltpu.make_async_remote_copy(
-                        src_ref=table_out,
-                        dst_ref=own_rows(0),
-                        send_sem=send_row.at[dy + OUT],
-                        recv_sem=row_sem,
-                        device_id=device(dy, across(dx)),
-                        device_id_type=MESH,
-                    ).start()
-                    return _
-
-                lax.fori_loop(1 if dy == 0 else 0, NX, send_rows, 0)
+            plane_out[0] = jnp.max(hub_in[...], axis=0)
+            pltpu.make_async_copy(plane_out.at[0], tops.at[0], tops_sem).start()
+
+            def send_tops(step, _):
+                pltpu.make_async_remote_copy(
+                    src_ref=plane_out.at[0],
+                    dst_ref=tops.at[0],
+                    send_sem=send_top,
+                    recv_sem=tops_sem,
+                    device_id=(lax.rem(me + step, EP), tp),
+                    device_id_type=MESH,
+                ).start()
+                return _
+
+            lax.fori_loop(1, EP, send_tops, 0)
+
+    def own_rows(dy):
+        return table.at[pl.ds(lax.rem(here_y + (NY + dy), NY) * NX, NX)]
+
+    reached = [dy for dy in range(-OUT, OUT + 1) if dy != 0]
+
+    def spread_rows():
+        pltpu.make_async_copy(own_rows(0), own_rows(0), scale_sem).wait()
+        for dy in reached:
+            pltpu.make_async_remote_copy(
+                src_ref=own_rows(0),
+                dst_ref=own_rows(0),
+                send_sem=send_row,
+                recv_sem=row_sem,
+                device_id=device(dy, here_x),
+                device_id_type=MESH,
+            ).start()
 
     passed = [(-OUT, step) for step in range(1, NY // 2 - OUT + 1)]
     passed += [(OUT, -step) for step in range(1, (NY - 1) // 2 - OUT + 1)]
@@ -276,7 +317,7 @@
         )
 
     def pass_rows():
-        near = table.at[pl.ds(0, (2 * OUT + 1) * NX)]
+        near = table.at[pl.ds(0, len(reached) * NX)]
         pltpu.make_async_copy(near, near, row_sem).wait()
         for dy, step in passed:
             pass_copy(dy, step).start()
@@ -364,14 +405,14 @@
             return _
 
         pairs = list(enumerate(serves))
-        far, rest = pairs[:far_count], pairs[far_count:]
-        far, rest = ((far + rest, rest), (far[:2], []), (far[2:] + rest, rest))[part]
-        far = [pair for pair in far if pair not in rest]
-        lax.fori_loop(0, NX, functools.partial(pick, pairs=far), 0)
-        for first in range(0, len(far), 2):
-            lax.fori_loop(0, NX, functools.partial(send_in_one, pairs=far[first : first + 2]), 0)
-        if not rest:
+        groups = [pairs[first : first + 2] for first in range(0, far_count, 2)]
+        groups = (groups, groups[:1], groups[1:])[part]
+        for group in groups:
+            lax.fori_loop(0, NX, functools.partial(pick, pairs=group), 0)
+            lax.fori_loop(0, NX, functools.partial(send_in_one, pairs=group), 0)
+        if part == 1:
             return
+        rest = pairs[far_count:]
         lax.fori_loop(0, NX, functools.partial(pick, pairs=rest), 0)
         lax.fori_loop(1, NX, functools.partial(send_in_one, pairs=rest), 0)
         for at, (k, _dy) in pairs[far_count:]:
@@ -389,8 +430,10 @@
             find_largest()
         if turn == 2:
             meet_hubs()
+        if turn == 3:
+            spread_rows()
         if turn == 4:
-            spread_rows()
+            spread_tops()
         if turn == count + LAST - 1:
             pass_rows()
         while held_back:
@@ -409,8 +452,15 @@
 
     passing = table.at[pl.ds(0, len(passed) * NX)]
     pltpu.make_async_copy(passing, passing, pass_sem).wait()
+    pltpu.make_async_copy(tops, tops, tops_sem).wait()
+    lane = lax.broadcasted_iota(jnp.int32, (1, BLOCK), 1)
     for slot in range(2):
-        rows_ref[slot] = table[slot_ref[2 * me + slot]]
+        expert = slot_ref[2 * me + slot]
+        largest = jnp.max(jnp.where(lane == expert, tops[0], 0.0))
+        largest_ref[slot] = jnp.full((1, BLOCK), largest, jnp.float32)
+        bound = jnp.full((row_blocks, BLOCK), largest, jnp.float32) + EPSILON
+        scale = jnp.broadcast_to(to_column(table[expert], row_blocks), (row_blocks, BLOCK))
+        factors_ref[slot] = (scale * (1.0 / math.sqrt(BLOCK))) / bound
     for stage in range(STAGES):
         part = raw_ref.at[:, pl.ds(0, EP * PIECES[stage])]
         pltpu.make_async_copy(part, part, in_sem.at[stage]).wait()
@@ -434,9 +484,13 @@
     def _():
         sent = hub_in.at[pl.ds(0, tp_size - 1)]
         pltpu.make_async_copy(sent, sent, send_hub).wait()
-        for dy in range(-OUT, OUT + 1):
-            sent = hub_in.at[pl.ds(0, NX - 1 if dy == 0 else NX)]
-            pltpu.make_async_copy(sent, sent, send_row.at[dy + OUT]).wait()
+        sent = gathered.at[pl.ds(0, EP - 1)]
+        pltpu.make_async_copy(sent, sent, send_top).wait()
+
+    sent = table.at[pl.ds(0, NX - 1)]
+    pltpu.make_async_copy(sent, sent, send_scale).wait()
+    sent = table.at[pl.ds(0, len(reached) * NX)]
+    pltpu.make_async_copy(sent, sent, send_row).wait()
 
 
 def move_rows(tp_size, stored, scale, slot_expert):
@@ -448,23 +502,28 @@
         out_shape=(
             jax.ShapeDtypeStruct((2, rows, BLOCK), jnp.bfloat16),
             jax.ShapeDtypeStruct((2, 1, BLOCK), jnp.float32),
+            jax.ShapeDtypeStruct((2, row_blocks, BLOCK), jnp.float32),
+            jax.ShapeDtypeStruct((BLOCK, BLOCK), jnp.bfloat16),
         ),
         in_specs=[pl.BlockSpec(memory_space=pltpu.HBM)] * 3,
         out_specs=(
             pl.BlockSpec(memory_space=pl.ANY),
+            pl.BlockSpec(memory_space=pltpu.VMEM),
+            pl.BlockSpec(memory_space=pltpu.VMEM),
             pl.BlockSpec(memory_space=pltpu.VMEM),
         ),
         scratch_shapes=[
             pltpu.SMEM(slot_expert.shape, jnp.int32),
             pltpu.VMEM(scale.shape, jnp.bfloat16),
             pltpu.VMEM((rows, BLOCK), jnp.bfloat16),
-            pltpu.VMEM((BLOCK, BLOCK), jnp.bfloat16),
             pltpu.VMEM((row_blocks, BLOCK), jnp.float32),
             pltpu.VMEM((1, 1, BLOCK), jnp.float32),
-            pltpu.VMEM((NX, 1, BLOCK), jnp.float32),
-            pltpu.VMEM((NX, 1, BLOCK), jnp.float32),
-            pltpu.VMEM((tp_size, NX, 1, BLOCK), jnp.float32),
-            pltpu.VMEM((NX, 1, BLOCK), jnp.float32),
+            pltpu.VMEM((1, 1, BLOCK), jnp.float32),
+            pltpu.VMEM((EP, 1, BLOCK), jnp.float32),
+            pltpu.VMEM((1, 1, BLOCK), jnp.float32),
+            pltpu.VMEM((tp_size, 1, BLOCK), jnp.float32),
+            pltpu.VMEM((1, 1, BLOCK), jnp.float32),
+            pltpu.VMEM((1, 1, BLOCK), jnp.float32),
             pltpu.VMEM((EP, 1, BLOCK), jnp.float32),
             dma,
             dma((2,)),
@@ -477,12 +536,16 @@
             dma,
             dma,
             dma,
+            dma,
+            dma,
+            dma,
+            dma,
             dma((HOLD, len(STEPS))),
             dma((HOLD, len(STEPS))),
             dma((STAGES,)),
             dma,
             dma,
-            dma((2 * OUT + 1,)),
+            dma,
             dma,
             pltpu.SemaphoreType.REGULAR,
         ]
@@ -498,24 +561,17 @@
 TILE = 1024
 
 
-def finish_kernel(raw_ref, rows_ref, out_ref, largest_ref, staged, factors, sems):
+def finish_kernel(raw_ref, tops_ref, factors_ref, signs_ref, out_ref, largest_ref, staged, sems):
     count, rows, _ = staged.shape
-    row_blocks = rows // BLOCK
     blocks = TILE // BLOCK
-    signs = sign_matrix()
-    lane = lax.broadcasted_iota(jnp.int32, (1, BLOCK), 1)
     copies = []
     for slot in range(count):
-        row = rows_ref[slot]
-        largest = jnp.max(jnp.where(lane < row_blocks, 0.0, row))
-        largest_ref[slot] = largest
-        bound = jnp.full((row_blocks, BLOCK), largest, jnp.float32) + EPSILON
-        scale = jnp.broadcast_to(to_column(row, row_blocks), (row_blocks, BLOCK))
-        factors[slot] = (scale * (1.0 / math.sqrt(BLOCK))) / bound
         for tile in range(rows // TILE):
             at = pl.ds(tile * TILE, TILE)
-            turned = jnp.dot(raw_ref[slot, at, :], signs, preferred_element_type=jnp.float32)
-            factor = factors[slot, pl.ds(tile * blocks, blocks), :]
+            turned = jnp.dot(
+                raw_ref[slot, at, :], signs_ref[...], preferred_element_type=jnp.float32
+            )
+            factor = factors_ref[slot, pl.ds(tile * blocks, blocks), :]
             scaled = turned.reshape(blocks, BLOCK, BLOCK) * factor[:, None, :]
             staged[slot, at, :] = scaled.reshape(TILE, BLOCK).astype(jnp.bfloat16)
             copy = pltpu.make_async_copy(
@@ -523,11 +579,13 @@
             )
             copy.start()
             copies.append(copy)
+    for slot in range(count):
+        largest_ref[slot] = jnp.max(tops_ref[slot])
     for copy in copies:
         copy.wait()
 
 
-def finish(raw, rows):
+def finish(raw, tops, factors, signs):
     count, height, width = raw.shape
     return pl.pallas_call(
         finish_kernel,
@@ -535,30 +593,25 @@
             jax.ShapeDtypeStruct(raw.shape, jnp.bfloat16),
             jax.ShapeDtypeStruct((count,), jnp.float32),
         ),
-        in_specs=[
-            pl.BlockSpec(memory_space=pltpu.VMEM),
-            pl.BlockSpec(memory_space=pltpu.VMEM),
-        ],
+        in_specs=[pl.BlockSpec(memory_space=pltpu.VMEM)] * 4,
         out_specs=(
             pl.BlockSpec(memory_space=pltpu.HBM),
             pl.BlockSpec(memory_space=pltpu.SMEM),
         ),
         scratch_shapes=[
             pltpu.VMEM(raw.shape, jnp.bfloat16),
-            pltpu.VMEM((count, height // BLOCK, BLOCK), jnp.float32),
             pltpu.SemaphoreType.DMA((count, height // TILE)),
         ],
         compiler_params=pltpu.CompilerParams(vmem_limit_bytes=VMEM_LIMIT),
         name="finish",
-    )(raw, rows)
+    )(raw, tops, factors, signs)
 
 
 def on_device(tp_size, quantized, block_scale, slot_expert):
     rows = quantized.shape[1]
     stored = quantized.reshape(rows, BLOCK)
     scale = block_scale.reshape(1, rows // BLOCK)
-    raw, picked_rows = move_rows(tp_size, stored, scale, slot_expert)
-    return finish(raw, picked_rows)
+    return finish(*move_rows(tp_size, stored, scale, slot_expert))
 
 
 def solution(mesh):

time: 73.3 us -> 73.1 us (level)
  no operation moved by 1% of the time
where the time goes in v4:
time: 73.1 us; the launch traced here: 72.9 us
  Pallas kernels  72.2 us (99%)
    pallas_call x1, Pallas kernels, move_rows(): pl.pallas_call(functools.partial(move_kernel, tp_size), out_shape=(jax.Sh...  70 us
    pallas_call x1, Pallas kernels, finish(): pl.pallas_call(finish_kernel, out_shape=(jax.ShapeDtypeStruct(raw.shape,...  2.19 us

profile of v4, /device:TPU:6, one launch (start us, length us, event | category | flops | bytes accessed | tf_op | source)
XLA Modules:
  0.0 72.9 jit_solution(12532846839496291106)
XLA Ops:
  0.6 70.0 %move_rows.1 = (bf16[2,4096,128]{2,1,0:T(8,128)(2,1)S(1)}, f32[2,1,128]{2,1,0:T(1,128)S(1)}, f32[2,32,128]{2,1,0:T(8,128)S(1)}, bf16[128,128]{1,0:T(8,128)(2,1)S(1)}) custom-call(s32[64]{0:T(128)} %slot_hbm.1, bf16[4096,128]{1,0:T(8,128)(2,1)} %bitcast.2, bf16[1,32]{1,0:T(2,128)(2,1)} %bitcast.3), custom_call_target="tpu_custom_call" | custom-call | tf_op jit(solution)/shard_map/move_rows/pallas_call | solution.py:500
  70.7 2.2 %finish.1 = (bf16[2,4096,128]{2,1,0:T(8,128)(2,1)}, f32[2]{0:T(128)}) custom-call(bf16[2,4096,128]{2,1,0:T(8,128)(2,1)S(1)} %get-tuple-element.6.raw_ref, f32[2,1,128]{2,1,0:T(1,128)S(1)} %get-tuple-element.7.tops_ref, f32[2,32,128]{2,1,0:T(8,128)S(1)} %get-tuple-element.8.factors_ref, bf16[128,128]{1,0:T(8,128)(2,1)S(1)} %get-tuple-element.9.signs_ref), custom_call_target="tpu_custom_call" | custom-call | tf_op jit(solution)/shard_map/finish/pallas_call | solution.py:590

commit v5 on v4

--- a/solution.py
+++ b/solution.py
@@ -437,7 +437,7 @@
         if turn == count + LAST - 1:
             pass_rows()
         while held_back:
-            serve(held_back.pop(), 2)
+            serve(held_back.pop(), 0)
         if turn >= LAST:
             step = turn - LAST
             right_copy(LAST - 1, step).wait_recv()
@@ -445,7 +445,6 @@
             stage, part = STEPS[step]
             if part == SUBS[stage] - 1:
                 if stage < STAGES - 1:
-                    serve(stage, 1)
                     held_back.append(stage)
                 else:
                     serve(stage, 0)

time: 73.1 us -> 72.9 us (level)
  no operation moved by 1% of the time
where the time goes in v5:
time: 72.9 us; the launch traced here: 72.6 us
  Pallas kernels  71.9 us (99%)
    pallas_call x1, Pallas kernels, move_rows(): pl.pallas_call(functools.partial(move_kernel, tp_size), out_shape=(jax.Sh...  69.7 us
    pallas_call x1, Pallas kernels, finish(): pl.pallas_call(finish_kernel, out_shape=(jax.ShapeDtypeStruct(raw.shape,...  2.19 us

profile of v5, /device:TPU:6, one launch (start us, length us, event | category | flops | bytes accessed | tf_op | source)
XLA Modules:
  0.0 72.6 jit_solution(14617593114431018453)
XLA Ops:
  0.6 69.7 %move_rows.1 = (bf16[2,4096,128]{2,1,0:T(8,128)(2,1)S(1)}, f32[2,1,128]{2,1,0:T(1,128)S(1)}, f32[2,32,128]{2,1,0:T(8,128)S(1)}, bf16[128,128]{1,0:T(8,128)(2,1)S(1)}) custom-call(s32[64]{0:T(128)} %slot_hbm.1, bf16[4096,128]{1,0:T(8,128)(2,1)} %bitcast.2, bf16[1,32]{1,0:T(2,128)(2,1)} %bitcast.3), custom_call_target="tpu_custom_call" | custom-call | tf_op jit(solution)/shard_map/move_rows/pallas_call | solution.py:499
  70.4 2.2 %finish.1 = (bf16[2,4096,128]{2,1,0:T(8,128)(2,1)}, f32[2]{0:T(128)}) custom-call(bf16[2,4096,128]{2,1,0:T(8,128)(2,1)S(1)} %get-tuple-element.6.raw_ref, f32[2,1,128]{2,1,0:T(1,128)S(1)} %get-tuple-element.7.tops_ref, f32[2,32,128]{2,1,0:T(8,128)S(1)} %get-tuple-element.8.factors_ref, bf16[128,128]{1,0:T(8,128)(2,1)S(1)} %get-tuple-element.9.signs_ref), custom_call_target="tpu_custom_call" | custom-call | tf_op jit(solution)/shard_map/finish/pallas_call | solution.py:589
